TPU v7x, 512 devices: a whole 4x8x8 slice. The times are simulated.
512 devices in a mesh: row: 32 (over z, y_hi), col: 16 (over y_lo, x, core).
Axes of the slice: x: 4, y: 8 (y_hi: 4, y_lo: 2; y = y_hi * 2 + y_lo), z: 8, core: 2. Of those that a mesh axis runs over, the one named last changes fastest.
Arguments:
- signal: float32 [32, 65536], P(None, 'row'), may hold values from -8 to 8
- tile_values: bfloat16 [32, 16, 64, 128, 128], P('row', 'col'), may hold values from 1e-12 to 1, as said below
- tile_places: int32 [32, 16, 2, 64], P('row', 'col'), may hold values from 0 to 31, as said below
- tile_counts: int32 [32, 16], P('row', 'col'), may hold values from 16 to 64, as said below
Outputs:
- first_wavelet: float32 [32, 65536], P(None, 'row')
- second_wavelet: float32 [32, 65536], P(None, 'row')
- lowpass: float32 [32, 65536], P(None, 'row')
Inputs may be any that keep to these rules, and one draw needn't show every extreme that they name: `tile_values`: A is symmetric, and every node's row of A has a positive entry on the diagonal. Slots at or after a device's count hold tiles that are not part of A. `tile_places`: place 0 lies below 16, place 1 below 32; the live slots of one device name distinct places. `tile_counts`: some device is full in every draw.
All inputs are finite; a program needn't handle non-finite values.
Results may differ from a plain program's by a relative error of at most 0.0003.
Values may be sent and summed in bfloat16 or wider, within the bound.
No kernel may reach another device: no remote copies, remote signals or barrier semaphores. Data moves between devices by JAX's collectives and lax.ppermute only.
A program may use at most 64 MiB of HBM per device.

v0:
```python
import jax
import jax.numpy as jnp
from jax import lax
from jax.sharding import PartitionSpec as P

highest_precision = lax.Precision.HIGHEST


def broadcast(block, axis, holder):
    block = jnp.where(lax.axis_index(axis) == holder, block, jnp.zeros_like(block))
    return lax.psum(block, axis)


def on_device(signal, tile_values, tile_places, tile_counts):
    channels, row_len = signal.shape
    slot_count = tile_values.shape[2]
    tile_width = tile_values.shape[3]
    tile_rows = row_len // tile_width
    row_size = lax.axis_size("row")
    col_size = lax.axis_size("col")
    halves = row_size // col_size
    blocks = tile_values.reshape(slot_count, tile_width, tile_width)
    places = tile_places.reshape(2, slot_count)
    live_count = tile_counts.reshape(())
    live_slot = (lax.iota(jnp.int32, slot_count) < live_count).astype(jnp.float32)
    row_hot = (places[0][:, None] == lax.iota(jnp.int32, tile_rows)[None, :]).astype(
        jnp.float32
    ) * live_slot[:, None]

    def over_slots(partial_of):
        return partial_of(0, slot_count)

    def degree_part(start, size):
        sums = jnp.sum(blocks, axis=2, dtype=jnp.float32)
        return jnp.einsum("kt,ka->ta", row_hot, sums, precision=highest_precision)

    degree = lax.psum(over_slots(degree_part).reshape(row_len), "col")

    def walk(vector):
        scaled = (vector / degree[None, :]).astype(jnp.bfloat16)
        col_index = lax.axis_index("col")
        pieces = []
        for portion in range(halves):
            pieces.append(broadcast(scaled, "row", col_index * halves + portion))
        column = jnp.concatenate(pieces, axis=1).reshape(channels, halves * tile_rows, tile_width)

        def row_part(start, size):
            picked = jnp.take(column, places[1], axis=1)
            products = jnp.einsum(
                "kab,ckb->cka", blocks, picked, preferred_element_type=jnp.float32
            )
            return jnp.einsum("cka,kt->cta", products, row_hot, precision=highest_precision)

        partial_value = over_slots(row_part)
        spread = lax.psum(partial_value.reshape(channels, row_len), "col")
        return 0.5 * (vector + spread)

    walked = walk(signal)
    lowpass = walk(walked)
    return (jnp.abs(signal - walked), jnp.abs(walked - lowpass), lowpass)


def solution(mesh):
    in_specs = (
        P(None, "row"),
        P("row", "col", None, None, None),
        P("row", "col", None, None),
        P("row", "col"),
    )
    out_specs = (P(None, "row"), P(None, "row"), P(None, "row"))
    return jax.shard_map(
        on_device, mesh=mesh, in_specs=in_specs, out_specs=out_specs, check_vma=False
    )
```

profile of v0, /device:TPU:1, one launch (start us, length us, event | category | flops | bytes accessed | tf_op | source)
XLA Modules:
  0.0 942.9 jit_solution(6482408230794167764)
XLA Ops:
  7.2 0.0 copy-start.3
  7.2 0.0 copy-start.1
  7.2 0.0 all-reduce.13.cloned.1.call-start
  7.9 0.7 slice_bitcast_fusion
  8.6 0.0 copy-start
  8.6 2.4 convert_reduce_fusion
  11.0 0.1 convolution_bitcast_fusion
  11.1 33.8 %psum.49 = f32[2048]{0:T(1024)S(1)} all-reduce(f32[2048]{0:T(1024)S(1)} %convolution_bitcast_fusion), channel_id=1, replica_groups=mesh['row'=32,'col'=16] {'col'}, use_global_device_ids=true, to_apply=%region_1.0 | all-reduce | flops 2048 | bytes 16384 | tf_op jit(solution)/shard_map/psum | solution.py:37
  45.0 0.0 copy-done.1
  45.0 0.7 broadcast_select_fusion.3
  45.7 0.0 all-reduce.13.cloned.1.call-update
  45.7 0.0 all-reduce.7.cloned.1.call-start
  45.8 0.0 copy-done.3
  45.8 293.4 %all-reduce.13.cloned.1.call-done = (bf16[32,2048]{1,0:T(8,128)(2,1)}, bf16[32,2048]{1,0:T(8,128)(2,1)}) async-done(((bf16[32,2048]{1,0:T(8,128)(2,1)}, bf16[32,2048]{1,0:T(8,128)(2,1)}), (bf16[32,2048]{1,0:T(8,128)(2,1)}, bf16[32,2048]{1,0:T(8,128)(2,1)})) %all-reduce.13.cloned.1.call-update) | async-done | bytes 262160 | tf_op jit(solution)/shard_map/psum | solution.py:11
  339.2 1.0 copy_bitcast_fusion.3
  340.2 0.7 gather_fusion
  340.9 0.0 copy-done
  340.9 1.2 fusion.4
  342.1 1.2 fusion.12
  343.3 0.8 copy.24
  344.1 0.0 all-reduce.7.cloned.1.call-update
  344.1 0.0 all-reduce.11.cloned.1.call-start
  344.2 143.4 %all-reduce.7.cloned.1.call-done = f32[32,2048]{1,0:T(8,128)} async-done(((f32[32,2048]{1,0:T(8,128)}), f32[32,2048]{1,0:T(8,128)}) %all-reduce.7.cloned.1.call-update) | async-done | bytes 262160 | tf_op jit(solution)/shard_map/psum | solution.py:55
  487.5 1.7 broadcast_select_fusion.2
  489.2 0.7 broadcast_select_fusion
  489.9 0.0 all-reduce.11.cloned.1.call-update
  489.9 0.0 all-reduce.9.cloned.1.call-start
  489.9 296.2 %all-reduce.11.cloned.1.call-done = (bf16[32,2048]{1,0:T(8,128)(2,1)}, bf16[32,2048]{1,0:T(8,128)(2,1)}) async-done(((bf16[32,2048]{1,0:T(8,128)(2,1)}, bf16[32,2048]{1,0:T(8,128)(2,1)}), (bf16[32,2048]{1,0:T(8,128)(2,1)}, bf16[32,2048]{1,0:T(8,128)(2,1)})) %all-reduce.11.cloned.1.call-update) | async-done | bytes 262160 | tf_op jit(solution)/shard_map/psum | solution.py:11
  786.1 1.0 copy_bitcast_fusion.2
  787.1 0.7 gather_fusion.1
  787.8 0.0 copy-start.2
  787.8 1.2 fusion.7
  789.0 1.2 fusion.10
  790.2 0.8 copy.23
  791.0 0.0 all-reduce.9.cloned.1.call-update
  791.0 143.4 %all-reduce.9.cloned.1.call-done = f32[32,2048]{1,0:T(8,128)} async-done(((f32[32,2048]{1,0:T(8,128)}), f32[32,2048]{1,0:T(8,128)}) %all-reduce.9.cloned.1.call-update) | async-done | bytes 262160 | tf_op jit(solution)/shard_map/psum | solution.py:55
  934.4 0.0 copy-done.2
  934.4 1.9 subtract_abs_fusion
  (3 shorter events, 0.0 us)
Async XLA Ops:
  7.2 38.6 %copy-start.3 = (s32[1,1,2,64]{3,2,1,0:T(2,128)S(1)}, s32[1,1,2,64]{3,2,1,0:T(2,128)}, u32[]{:S(2)}) copy-start(s32[1,1,2,64]{3,2,1,0:T(2,128)} %param.8) | copy-start | bytes 1540
  7.2 37.8 %copy-start.1 = (f32[32,2048]{1,0:T(8,128)S(1)}, f32[32,2048]{1,0:T(8,128)}, u32[]{:S(2)}) copy-start(f32[32,2048]{1,0:T(8,128)} %param.6) | copy-start | bytes 786436
  7.2 332.0 %all-reduce.13.cloned.1.call-start = ((), (), s32[]{:S(2)}) async-start(), calls=%async_computation.3 | async-start | bytes 524288 | tf_op jit(solution)/shard_map/psum | solution.py:11
  8.6 332.3 %copy-start = (bf16[1,1,64,128,128]{4,3,2,1,0:T(8,128)(2,1)S(1)}, bf16[1,1,64,128,128]{4,3,2,1,0:T(8,128)(2,1)}, u32[]{:S(2)}) copy-start(bf16[1,1,64,128,128]{4,3,2,1,0:T(8,128)(2,1)} %param.7) | copy-start | bytes 6291460
  45.7 441.8 %all-reduce.7.cloned.1.call-start = ((), (), s32[]{:S(2)}) async-start(), calls=%async_computation | async-start | bytes 524288 | tf_op jit(solution)/shard_map/psum | solution.py:55
  344.1 442.0 %all-reduce.11.cloned.1.call-start = ((), (), s32[]{:S(2)}) async-start(), calls=%async_computation.2 | async-start | bytes 524288 | tf_op jit(solution)/shard_map/psum | solution.py:11
  489.9 444.5 %all-reduce.9.cloned.1.call-start = ((), (), s32[]{:S(2)}) async-start(), calls=%async_computation.1 | async-start | bytes 524288 | tf_op jit(solution)/shard_map/psum | solution.py:55
  787.8 146.7 %copy-start.2 = (f32[32,2048]{1,0:T(8,128)S(1)}, f32[32,2048]{1,0:T(8,128)}, u32[]{:S(2)}) copy-start(f32[32,2048]{1,0:T(8,128)} %all-reduce.7.cloned.1.call-done) | copy-start | bytes 786436
Sparse Core Ops, SparseCore 0:
  45.9 293.3 all-reduce.12
  344.3 143.2 all-reduce.6
  491.1 294.9 all-reduce.10
  791.1 143.2 all-reduce.8
where the time goes:
time: 943 us
  waiting for transfers between devices  876 us (93%)
  blocking collectives  33.8 us (4%)
  between operations  14.6 us (2%)
    psum x2, waiting for transfers between devices, broadcast(): return lax.psum(block, axis)  590 us
    psum x2, waiting for transfers between devices, walk(): spread = lax.psum(partial_value.reshape(channels, row_len), 'col')  287 us
    psum x1, blocking collectives, on_device(): degree = lax.psum(over_slots(degree_part).reshape(row_len), 'col')  33.8 us
  transfers between devices with their start and end apart: 4, of which 4 were waited for; matrix products, arithmetic and copies ran while one was open for 0% of the time, Pallas kernels for 0%

commit v1 on v0

--- a/solution.py
+++ b/solution.py
@@ -52,7 +52,7 @@
             return jnp.einsum("cka,kt->cta", products, row_hot, precision=highest_precision)
 
         partial_value = over_slots(row_part)
-        spread = lax.psum(partial_value.reshape(channels, row_len), "col")
+        spread = jnp.sum(lax.all_gather(partial_value.reshape(channels, row_len), "col"), axis=0)
         return 0.5 * (vector + spread)
 
     walked = walk(signal)

time: 943 us -> 777 us (0.82)
  waiting for transfers between devices: 876 us -> 707 us
    psum x2 -> x0, waiting for transfers between devices: 287 us -> none  [walk(): spread = lax.psum(partial_value.reshape(channels, row_len), 'col')]
    all_gather x0 -> x2, waiting for transfers between devices: none -> 120 us  [walk(): lax.all_gather(partial_value.reshape(channels, row_len), 'col')]
where the time goes in v1:
time: 777 us
  waiting for transfers between devices  707 us (91%)
  blocking collectives  33.8 us (4%)
  between operations  14.6 us (2%)
  other arithmetic  12.3 us (2%)
    psum x2, waiting for transfers between devices, broadcast(): return lax.psum(block, axis)  587 us
    all_gather x2, waiting for transfers between devices, walk(): lax.all_gather(partial_value.reshape(channels, row_len), 'col')  120 us
    psum x1, blocking collectives, on_device(): degree = lax.psum(over_slots(degree_part).reshape(row_len), 'col')  33.8 us
  transfers between devices with their start and end apart: 4, of which 4 were waited for; matrix products, arithmetic and copies ran while one was open for 0% of the time, Pallas kernels for 0%

profile of v1, /device:TPU:1, one launch (start us, length us, event | category | flops | bytes accessed | tf_op | source)
XLA Modules:
  0.0 776.6 jit_solution(13378843212571152486)
XLA Ops:
  7.2 0.0 copy-start.2
  7.2 0.0 copy-start.1
  7.2 0.0 all-reduce.7.cloned.1.call-start
  7.9 0.7 slice_bitcast_fusion
  8.6 0.0 copy-start
  8.6 2.4 convert_reduce_fusion
  11.0 0.1 convolution_bitcast_fusion.2
  11.1 33.8 %psum.35 = f32[2048]{0:T(1024)S(1)} all-reduce(f32[2048]{0:T(1024)S(1)} %convolution_bitcast_fusion.2), channel_id=1, replica_groups=mesh['row'=32,'col'=16] {'col'}, use_global_device_ids=true, to_apply=%region_1.0 | all-reduce | flops 2048 | bytes 16384 | tf_op jit(solution)/shard_map/psum | solution.py:37
  45.0 0.0 copy-done.1
  45.0 0.7 broadcast_select_fusion.3
  45.7 0.0 all-reduce.7.cloned.1.call-update
  45.7 0.0 all-gather.3.cloned.1.call-start
  45.8 0.0 copy-done.2
  45.8 293.4 %all-reduce.7.cloned.1.call-done = (bf16[32,2048]{1,0:T(8,128)(2,1)}, bf16[32,2048]{1,0:T(8,128)(2,1)}) async-done(((bf16[32,2048]{1,0:T(8,128)(2,1)}, bf16[32,2048]{1,0:T(8,128)(2,1)}), (bf16[32,2048]{1,0:T(8,128)(2,1)}, bf16[32,2048]{1,0:T(8,128)(2,1)})) %all-reduce.7.cloned.1.call-update) | async-done | bytes 262160 | tf_op jit(solution)/shard_map/psum | solution.py:11
  339.2 1.0 copy_bitcast_fusion.1
  340.2 0.7 gather_fusion
  340.9 0.0 copy-done
  340.9 1.2 fusion.4
  342.1 1.2 convolution_bitcast_fusion.1
  343.3 0.7 all_gather_reshape.6
  344.1 0.0 all-gather.3.cloned.1.call-update
  344.1 0.0 all-reduce.5.cloned.1.call-start
  344.1 59.9 %all-gather.3.cloned.1.call-done = f32[16,32,2048]{2,1,0:T(8,128)} async-done(((f32[1,32,2048]{2,1,0:T(8,128)}), f32[16,32,2048]{2,1,0:T(8,128)}) %all-gather.3.cloned.1.call-update) | async-done | bytes 4194320 | tf_op jit(solution)/shard_map/all_gather | solution.py:55
  404.0 2.4 reduce_sum.28
  406.5 0.7 broadcast_select_fusion.2
  407.2 0.7 broadcast_select_fusion
  407.8 0.0 all-reduce.5.cloned.1.call-update
  407.9 0.0 all-gather.5.cloned.1.call-start
  407.9 294.0 %all-reduce.5.cloned.1.call-done = (bf16[32,2048]{1,0:T(8,128)(2,1)}, bf16[32,2048]{1,0:T(8,128)(2,1)}) async-done(((bf16[32,2048]{1,0:T(8,128)(2,1)}, bf16[32,2048]{1,0:T(8,128)(2,1)}), (bf16[32,2048]{1,0:T(8,128)(2,1)}, bf16[32,2048]{1,0:T(8,128)(2,1)})) %all-reduce.5.cloned.1.call-update) | async-done | bytes 262160 | tf_op jit(solution)/shard_map/psum | solution.py:11
  701.9 1.0 copy_bitcast_fusion
  702.9 0.7 gather_fusion.1
  703.6 1.2 fusion.7
  704.8 1.2 convolution_bitcast_fusion
  706.0 0.7 all_gather_reshape.7
  706.8 0.0 all-gather.5.cloned.1.call-update
  706.8 59.9 %all-gather.5.cloned.1.call-done = f32[16,32,2048]{2,1,0:T(8,128)} async-done(((f32[1,32,2048]{2,1,0:T(8,128)}), f32[16,32,2048]{2,1,0:T(8,128)}) %all-gather.5.cloned.1.call-update) | async-done | bytes 4194320 | tf_op jit(solution)/shard_map/all_gather | solution.py:55
  766.7 2.4 reduce_sum.29
  769.1 0.9 subtract_abs_fusion
  (3 shorter events, 0.0 us)
Async XLA Ops:
  7.2 38.6 %copy-start.2 = (s32[1,1,2,64]{3,2,1,0:T(2,128)S(1)}, s32[1,1,2,64]{3,2,1,0:T(2,128)}, u32[]{:S(2)}) copy-start(s32[1,1,2,64]{3,2,1,0:T(2,128)} %param.8) | copy-start | bytes 1540
  7.2 37.8 %copy-start.1 = (f32[32,2048]{1,0:T(8,128)S(1)}, f32[32,2048]{1,0:T(8,128)}, u32[]{:S(2)}) copy-start(f32[32,2048]{1,0:T(8,128)} %param.6) | copy-start | bytes 786436
  7.2 332.0 %all-reduce.7.cloned.1.call-start = ((), (), s32[]{:S(2)}) async-start(), calls=%async_computation.3 | async-start | bytes 524288 | tf_op jit(solution)/shard_map/psum | solution.py:11
  8.6 332.3 %copy-start = (bf16[1,1,64,128,128]{4,3,2,1,0:T(8,128)(2,1)S(1)}, bf16[1,1,64,128,128]{4,3,2,1,0:T(8,128)(2,1)}, u32[]{:S(2)}) copy-start(bf16[1,1,64,128,128]{4,3,2,1,0:T(8,128)(2,1)} %param.7) | copy-start | bytes 6291460
  45.7 358.3 %all-gather.3.cloned.1.call-start = ((), (), s32[]{:S(2)}) async-start(), calls=%async_computation | async-start | bytes 4456448 | tf_op jit(solution)/shard_map/all_gather | solution.py:55
  344.1 357.8 %all-reduce.5.cloned.1.call-start = ((), (), s32[]{:S(2)}) async-start(), calls=%async_computation.2 | async-start | bytes 524288 | tf_op jit(solution)/shard_map/psum | solution.py:11
  407.9 358.9 %all-gather.5.cloned.1.call-start = ((), (), s32[]{:S(2)}) async-start(), calls=%async_computation.1 | async-start | bytes 4456448 | tf_op jit(solution)/shard_map/all_gather | solution.py:55
Sparse Core Ops, SparseCore 0:
  45.9 293.3 all-reduce.6
  344.2 59.7 all-gather.2
  408.0 293.8 all-reduce.4
  706.9 59.7 all-gather.4
